TPU v7x, 32 devices: a whole 2x2x4 slice. The times are simulated.
32 devices in a mesh: groups: 2 (over y), slices: 8 (over z, x), ering: 2 (over core).
Axes of the slice: x: 2, y: 2, z: 4, core: 2. Of those that a mesh axis runs over, the one named last changes fastest.
Arguments:
- positions: float32 [3, 128, 256], P(None, ('groups', 'slices'), 'ering'), parts along dimension 1, may hold values from -9 to 9
- hidden: bfloat16 [128, 256, 256], P(('groups', 'slices'), 'ering'), parts along dimension 0, may hold values from -6 to 6
- cotangent: bfloat16 [128, 256, 256], P(('groups', 'slices'), 'ering'), parts along dimension 0, may hold values from -6 to 6
- embed_weight: float32 [32, 4], replicated, may hold values from -3 to 3
- embed_bias: float32 [32], replicated, may hold values from -3 to 3
- pair_weight: bfloat16 [32, 32], replicated, may hold values from -1 to 1
- pair_bias: float32 [32], replicated, may hold values from -3 to 3
- one_weight: bfloat16 [256, 256], replicated, may hold values from -0.375 to 0.375
- pool_weight: bfloat16 [32, 256], replicated, may hold values from -1 to 1
- mean_weight: bfloat16 [256, 256], replicated, may hold values from -0.375 to 0.375
- one_bias: float32 [256], replicated, may hold values from -3 to 3
- drift_weight: bfloat16 [3, 256], replicated, may hold values from -0.375 to 0.375
Outputs:
- updated: bfloat16 [128, 256, 256], P(('groups', 'slices'), 'ering'), parts along dimension 0
- hidden_grad: bfloat16 [128, 256, 256], P(('groups', 'slices'), 'ering'), parts along dimension 0
- link_terms: float32 [128, 256], P(('groups', 'slices'), 'ering'), parts along dimension 0
- pair_grad: float32 [64, 32], P('groups'), parts along dimension 0
- bias_grad: float32 [64], P('groups'), parts along dimension 0
- one_grad: float32 [512, 256], P('groups'), parts along dimension 0
- pool_grad: float32 [64, 256], P('groups'), parts along dimension 0
- mean_grad: float32 [512, 256], P('groups'), parts along dimension 0
There are 2 independent parts, one for each index of `groups`. A program takes and returns all parts, laid end to end along the dimension named above; an argument that names none is the same for every part. Nothing has to cross between parts.
All inputs are finite; a program needn't handle non-finite values.
Results may differ from a plain program's by a relative error of at most 0.0054.
Values may be sent and summed in bfloat16 or wider, within the bound.
No kernel may reach another device: no remote copies, remote signals or barrier semaphores. Data moves between devices by JAX's collectives and lax.ppermute only.
A program may use at most 64 MiB of HBM per device.

v0:
```python
import math
import jax
import jax.numpy as jnp
from jax import lax
from jax.sharding import PartitionSpec as P

HIGH = lax.Precision.HIGHEST
step_tau = 0.5


def from_behind(array, axis, by):
    size = lax.axis_size(axis)
    pairs = [(i, i + by) for i in range(size) if 0 <= i + by < size]
    return lax.ppermute(array, axis, pairs)


def local(
    positions,
    hidden,
    cotangent,
    embed_weight,
    embed_bias,
    pair_weight,
    pair_bias,
    one_weight,
    pool_weight,
    mean_weight,
    one_bias,
    drift_weight,
):
    own_count = hidden.shape[1]
    total_count = own_count * lax.axis_size("ering")
    slab_count = hidden.shape[0]
    scale = 1.0 / math.sqrt(slab_count * lax.axis_size("slices") * total_count)
    every_pos = lax.all_gather(positions, "ering", axis=2, tiled=True)
    full_rows = lax.all_gather(hidden, "ering", axis=1, tiled=True)
    mean_rows = (jnp.sum(full_rows.astype(jnp.float32), axis=1) / total_count).astype(jnp.bfloat16)

    def one_slice(carry, inputs):
        own_pos, all_pos, hid_s, cot_s, mean_s = inputs
        offsets = own_pos[:, :, None] - all_pos[:, None, :]
        radial = jnp.sqrt(jnp.sum(offsets * offsets, axis=0) + 1.0)
        features = jnp.concatenate([offsets, radial[None]], axis=0)
        pair_in = jnp.tanh(
            jnp.einsum("ck,kij->cij", embed_weight, features, precision=HIGH)
            + embed_bias[:, None, None]
        ).astype(jnp.bfloat16)
        pair_pre = (
            jnp.einsum("ck,kij->cij", pair_weight, pair_in, preferred_element_type=jnp.float32)
            + pair_bias[:, None, None]
        )
        pair_act = jnp.tanh(pair_pre)
        pooled = jnp.mean(pair_act + pair_in.astype(jnp.float32), axis=2).T.astype(jnp.bfloat16)
        one_pre = jnp.dot(hid_s, one_weight, preferred_element_type=jnp.float32)
        one_pre = one_pre + jnp.dot(pooled, pool_weight, preferred_element_type=jnp.float32)
        one_pre = (
            one_pre
            + jnp.dot(mean_s[None, :], mean_weight, preferred_element_type=jnp.float32)
            + one_bias
        )
        one_act = jnp.tanh(one_pre)
        updated = (one_act + hid_s.astype(jnp.float32)).astype(jnp.bfloat16)
        pre_grad = (cot_s.astype(jnp.float32) * (1.0 - one_act * one_act)).astype(jnp.bfloat16)
        column_part = jnp.sum(pre_grad.astype(jnp.float32), axis=0)
        pooled_grad = jnp.dot(pre_grad, pool_weight.T, preferred_element_type=jnp.float32)
        partial_grad = cot_s.astype(jnp.float32) + jnp.dot(
            pre_grad, one_weight.T, preferred_element_type=jnp.float32
        )
        act_grad = pooled_grad.T[:, :, None] / total_count * (1.0 - pair_act * pair_act)
        act_low = act_grad.astype(jnp.bfloat16)
        weight_term = jnp.einsum(
            "cij,kij->ck", act_low, pair_in, preferred_element_type=jnp.float32
        )
        bias_term = jnp.sum(act_grad, axis=(1, 2))
        carry = (
            carry[0] + weight_term,
            carry[1] + bias_term,
            carry[2] + jnp.einsum("id,ie->de", hid_s, pre_grad, preferred_element_type=jnp.float32),
            carry[3]
            + jnp.einsum("ic,ie->ce", pooled, pre_grad, preferred_element_type=jnp.float32),
        )
        return (carry, (updated, partial_grad, column_part))

    d_one = hidden.shape[2]
    p_width = pair_weight.shape[0]
    start = (
        jnp.zeros((p_width, p_width), jnp.float32),
        jnp.zeros((p_width,), jnp.float32),
        jnp.zeros((d_one, d_one), jnp.float32),
        jnp.zeros((p_width, d_one), jnp.float32),
    )
    inputs = (
        jnp.moveaxis(positions, 1, 0),
        jnp.moveaxis(every_pos, 1, 0),
        hidden,
        cotangent,
        mean_rows,
    )
    totals, (updated, partial_grad, column_parts) = lax.scan(one_slice, start, inputs)
    column_total = lax.psum(column_parts, "ering")
    mean_back = jnp.dot(column_total, mean_weight.astype(jnp.float32).T, precision=HIGH)
    hidden_grad = (partial_grad + mean_back[:, None, :] / total_count).astype(jnp.bfloat16)
    mean_term = jnp.dot(mean_rows.astype(jnp.float32).T, column_parts, precision=HIGH)
    grads = (totals[0], totals[1], totals[2], totals[3], mean_term)
    grads = lax.psum((grads[0], grads[1], grads[2], grads[3], grads[4]), ("slices", "ering"))
    drift = jnp.einsum(
        "cd,sid->csi", drift_weight.astype(jnp.float32), updated.astype(jnp.float32), precision=HIGH
    )
    first_next = from_behind(positions[:, :1, :], "slices", -1)
    following = jnp.concatenate([positions[:, 1:], first_next], axis=1)
    jump = following - positions - step_tau * drift
    link_terms = jnp.sum(jump * jump, axis=0) / (12.0 * step_tau)
    is_last = lax.axis_index("slices") == lax.axis_size("slices") - 1
    last_row = jnp.logical_and(is_last, jnp.arange(slab_count) == slab_count - 1)
    link_terms = jnp.where(last_row[:, None], jnp.float32(0.0), link_terms)
    return (
        updated,
        hidden_grad,
        link_terms,
        scale * grads[0],
        scale * grads[1],
        scale * grads[2],
        scale * grads[3],
        scale * grads[4],
    )


def solution(mesh):
    in_specs = (
        P(None, ("groups", "slices"), "ering"),
        P(("groups", "slices"), "ering", None),
        P(("groups", "slices"), "ering", None),
        P(),
        P(),
        P(),
        P(),
        P(),
        P(),
        P(),
        P(),
        P(),
    )
    out_specs = (
        P(("groups", "slices"), "ering", None),
        P(("groups", "slices"), "ering", None),
        P(("groups", "slices"), "ering"),
        P("groups", None),
        P("groups"),
        P("groups", None),
        P("groups", None),
        P("groups", None),
    )
    return jax.shard_map(local, mesh=mesh, in_specs=in_specs, out_specs=out_specs, check_vma=False)
```

profile of v0, /device:TPU:1, one launch (start us, length us, event | category | flops | bytes accessed | tf_op | source)
XLA Modules:
  0.0 349.7 jit_solution(2469969843966175401)
XLA Ops:
  12.8 8.3 %all-gather.2.cloned.1.call-done = bf16[8,256,256]{2,1,0:T(8,128)(2,1)} async-done(((bf16[8,128,256]{2,1,0:T(8,128)(2,1)}), bf16[8,256,256]{2,1,0:T(8,128)(2,1)}) %all-gather.2.cloned.1.call-update) | async-done | bytes 1048592 | tf_op jit(solution)/shard_map/all_gather | solution.py:36
  22.5 160.3 %while.23 = (s32[]{:T(128)}, f32[32,32]{1,0:T(8,128)S(1)}, f32[32]{0:T(128)S(1)}, f32[256,256]{1,0:T(8,128)S(1)}, f32[32,256]{1,0:T(8,128)S(1)}, /*index=5*/bf16...) while((s32[]{:T(128)}, f32[32,32]{1,0:T(8,128)S(1)}, ...), condition=%wide.region_6.7_spmd.clone, body=%wide.region_1.6_spmd.clone.sunk | while | flops 259163936 | bytes 40384416 | solution.py:99
  24.3 4.5 %tanh_convert_fusion.2 = bf16[128,256,32]{1,2,0:T(8,128)(2,1)S(1)} fusion(f32[32]{0:T(128)} %get-tuple-element.451, f32[1,128,256]{2,0,1:T(1,128)S(1)} %copy.37, f32[3,128,256]{2,0,1:T(4,128)S(1)} %get-tuple-element.385, f32[32,4]{0,1:T(4,128)} %get-tuple-element.450), kind=kOutput, calls=%fused_computation.6.clone.1 | convolution fusion | flops 52559872 | bytes 2622080 | tf_op jit(solution)/shard_map/while/body/eval_jaxpr/ck,kij->cij/dot_general | solution.py:45
  28.8 2.7 fusion.111
  33.3 3.5 fusion.115
  44.3 4.5 %tanh_convert_fusion.2 = bf16[128,256,32]{1,2,0:T(8,128)(2,1)S(1)} fusion(f32[32]{0:T(128)} %get-tuple-element.451, f32[1,128,256]{2,0,1:T(1,128)S(1)} %copy.37, f32[3,128,256]{2,0,1:T(4,128)S(1)} %get-tuple-element.385, f32[32,4]{0,1:T(4,128)} %get-tuple-element.450), kind=kOutput, calls=%fused_computation.6.clone.1 | convolution fusion | flops 52559872 | bytes 2622080 | tf_op jit(solution)/shard_map/while/body/eval_jaxpr/ck,kij->cij/dot_general | solution.py:45
  48.8 2.7 fusion.111
  53.3 3.5 fusion.115
  64.3 4.5 %tanh_convert_fusion.2 = bf16[128,256,32]{1,2,0:T(8,128)(2,1)S(1)} fusion(f32[32]{0:T(128)} %get-tuple-element.451, f32[1,128,256]{2,0,1:T(1,128)S(1)} %copy.37, f32[3,128,256]{2,0,1:T(4,128)S(1)} %get-tuple-element.385, f32[32,4]{0,1:T(4,128)} %get-tuple-element.450), kind=kOutput, calls=%fused_computation.6.clone.1 | convolution fusion | flops 52559872 | bytes 2622080 | tf_op jit(solution)/shard_map/while/body/eval_jaxpr/ck,kij->cij/dot_general | solution.py:45
  68.9 2.7 fusion.111
  73.3 3.5 fusion.115
  84.4 4.5 %tanh_convert_fusion.2 = bf16[128,256,32]{1,2,0:T(8,128)(2,1)S(1)} fusion(f32[32]{0:T(128)} %get-tuple-element.451, f32[1,128,256]{2,0,1:T(1,128)S(1)} %copy.37, f32[3,128,256]{2,0,1:T(4,128)S(1)} %get-tuple-element.385, f32[32,4]{0,1:T(4,128)} %get-tuple-element.450), kind=kOutput, calls=%fused_computation.6.clone.1 | convolution fusion | flops 52559872 | bytes 2622080 | tf_op jit(solution)/shard_map/while/body/eval_jaxpr/ck,kij->cij/dot_general | solution.py:45
  93.4 3.5 fusion.115
  104.4 4.5 %tanh_convert_fusion.2 = bf16[128,256,32]{1,2,0:T(8,128)(2,1)S(1)} fusion(f32[32]{0:T(128)} %get-tuple-element.451, f32[1,128,256]{2,0,1:T(1,128)S(1)} %copy.37, f32[3,128,256]{2,0,1:T(4,128)S(1)} %get-tuple-element.385, f32[32,4]{0,1:T(4,128)} %get-tuple-element.450), kind=kOutput, calls=%fused_computation.6.clone.1 | convolution fusion | flops 52559872 | bytes 2622080 | tf_op jit(solution)/shard_map/while/body/eval_jaxpr/ck,kij->cij/dot_general | solution.py:45
  113.4 3.5 fusion.115
  124.4 4.5 %tanh_convert_fusion.2 = bf16[128,256,32]{1,2,0:T(8,128)(2,1)S(1)} fusion(f32[32]{0:T(128)} %get-tuple-element.451, f32[1,128,256]{2,0,1:T(1,128)S(1)} %copy.37, f32[3,128,256]{2,0,1:T(4,128)S(1)} %get-tuple-element.385, f32[32,4]{0,1:T(4,128)} %get-tuple-element.450), kind=kOutput, calls=%fused_computation.6.clone.1 | convolution fusion | flops 52559872 | bytes 2622080 | tf_op jit(solution)/shard_map/while/body/eval_jaxpr/ck,kij->cij/dot_general | solution.py:45
  129.0 2.7 fusion.111
  133.4 3.5 fusion.115
  144.5 4.5 %tanh_convert_fusion.2 = bf16[128,256,32]{1,2,0:T(8,128)(2,1)S(1)} fusion(f32[32]{0:T(128)} %get-tuple-element.451, f32[1,128,256]{2,0,1:T(1,128)S(1)} %copy.37, f32[3,128,256]{2,0,1:T(4,128)S(1)} %get-tuple-element.385, f32[32,4]{0,1:T(4,128)} %get-tuple-element.450), kind=kOutput, calls=%fused_computation.6.clone.1 | convolution fusion | flops 52559872 | bytes 2622080 | tf_op jit(solution)/shard_map/while/body/eval_jaxpr/ck,kij->cij/dot_general | solution.py:45
  153.5 3.5 fusion.115
  164.5 4.5 %tanh_convert_fusion.2 = bf16[128,256,32]{1,2,0:T(8,128)(2,1)S(1)} fusion(f32[32]{0:T(128)} %get-tuple-element.451, f32[1,128,256]{2,0,1:T(1,128)S(1)} %copy.37, f32[3,128,256]{2,0,1:T(4,128)S(1)} %get-tuple-element.385, f32[32,4]{0,1:T(4,128)} %get-tuple-element.450), kind=kOutput, calls=%fused_computation.6.clone.1 | convolution fusion | flops 52559872 | bytes 2622080 | tf_op jit(solution)/shard_map/while/body/eval_jaxpr/ck,kij->cij/dot_general | solution.py:45
  173.5 3.5 fusion.115
  186.3 57.3 %all-reduce = (f32[32,32]{1,0:T(8,128)S(1)}, f32[32]{0:T(128)S(1)}, f32[32,256]{1,0:T(8,128)S(1)}) all-reduce(f32[32,32]{1,0:T(8,128)S(1)} %get-tuple-element.124, f32[32]{0:T(128)S(1)} %get-tuple-element.125, f32[32,256]{1,0:T(8,128)S(1)} %get-tuple-element.127), channel_id=1, replica_groups=mesh['groups'=2,'slices'=8,'ering'=2] {'slices','ering'}, use_global_device_ids=true, to_apply=%region_9.10 | all-reduce | flops 9248 | bytes 73984 | tf_op jit(solution)/shard_map/psum | solution.py:105
  250.6 90.4 %all-reduce.4.cloned.1.call-done = (f32[256,256]{1,0:T(8,128)}, f32[256,256]{1,0:T(8,128)}) async-done(((f32[256,256]{1,0:T(8,128)}, f32[256,256]{1,0:T(8,128)}), (f32[256,256]{1,0:T(8,128)}, f32[256,256]{1,0:T(8,128)})) %all-reduce.4.cloned.1.call-update) | async-done | bytes 524304 | tf_op jit(solution)/shard_map/psum | solution.py:105
  (273 shorter events, 103.2 us)
Async XLA Ops:
  7.2 239.3 %copy-start = (bf16[3,256]{1,0:T(4,128)(2,1)S(1)}, bf16[3,256]{1,0:T(4,128)(2,1)}, u32[]{:S(2)}) copy-start(bf16[3,256]{1,0:T(4,128)(2,1)} %param.25) | copy-start | bytes 4612
  7.2 13.9 %all-gather.2.cloned.1.call-start = ((), (), s32[]{:S(2)}) async-start(), calls=%async_computation | async-start | bytes 1572864 | tf_op jit(solution)/shard_map/all_gather | solution.py:36
  7.9 333.1 %all-reduce.4.cloned.1.call-start = ((), (), s32[]{:S(2)}) async-start(), calls=%async_computation.1 | async-start | bytes 1048576 | tf_op jit(solution)/shard_map/psum | solution.py:105
  8.7 237.8 %collective-permute-start = (f32[3,1,128]{2,0,1:T(4,128)S(1)}, f32[3,1,128]{2,0,1:T(4,128)S(1)}, u32[]{:S(2)}, u32[]{:S(2)}) collective-permute-start(f32[3,1,128]{2,0,1:T(4,128)S(1)} %slice.9), channel_id=1, source_target_pairs={{2,0},{4,2},{6,4},{8,6},{10,8},{12,10},{14,12},{3,1},{5,3},{7,5},{... | collective-permute-start | bytes 4616 | tf_op jit(solution)/shard_map/ppermute | solution.py:14
  22.5 224.0 %copy-start.6 = (f32[3,8,128]{2,1,0:T(8,128)S(1)}, f32[3,8,128]{2,1,0:T(8,128)}, u32[]{:S(2)}) copy-start(f32[3,8,128]{2,1,0:T(8,128)} %param.14) | copy-start | bytes 36868
  24.2 7.5 %copy-start.2 = (bf16[256,256]{1,0:T(8,128)(2,1)S(1)}, bf16[256,256]{1,0:T(8,128)(2,1)}, u32[]{:S(2)}) copy-start(bf16[256,256]{1,0:T(8,128)(2,1)} %get-tuple-element.447) | copy-start | bytes 393220 | tf_op jit(solution)/shard_map/while
  24.2 7.5 %copy-start.8 = (f32[256]{0:T(256)S(1)}, f32[256]{0:T(256)}, u32[]{:S(2)}) copy-start(f32[256]{0:T(256)} %get-tuple-element.457) | copy-start | bytes 3076 | tf_op jit(solution)/shard_map/while
  44.3 7.5 %copy-start.2 = (bf16[256,256]{1,0:T(8,128)(2,1)S(1)}, bf16[256,256]{1,0:T(8,128)(2,1)}, u32[]{:S(2)}) copy-start(bf16[256,256]{1,0:T(8,128)(2,1)} %get-tuple-element.447) | copy-start | bytes 393220 | tf_op jit(solution)/shard_map/while
  44.3 7.5 %copy-start.8 = (f32[256]{0:T(256)S(1)}, f32[256]{0:T(256)}, u32[]{:S(2)}) copy-start(f32[256]{0:T(256)} %get-tuple-element.457) | copy-start | bytes 3076 | tf_op jit(solution)/shard_map/while
  64.3 7.5 %copy-start.2 = (bf16[256,256]{1,0:T(8,128)(2,1)S(1)}, bf16[256,256]{1,0:T(8,128)(2,1)}, u32[]{:S(2)}) copy-start(bf16[256,256]{1,0:T(8,128)(2,1)} %get-tuple-element.447) | copy-start | bytes 393220 | tf_op jit(solution)/shard_map/while
  64.3 7.5 %copy-start.8 = (f32[256]{0:T(256)S(1)}, f32[256]{0:T(256)}, u32[]{:S(2)}) copy-start(f32[256]{0:T(256)} %get-tuple-element.457) | copy-start | bytes 3076 | tf_op jit(solution)/shard_map/while
  84.3 7.3 %copy-start.4 = (bf16[32,256]{1,0:T(8,128)(2,1)S(1)}, bf16[32,256]{1,0:T(8,128)(2,1)}, u32[]{:S(2)}) copy-start(bf16[32,256]{1,0:T(8,128)(2,1)} %get-tuple-element.454) | copy-start | bytes 49156 | tf_op jit(solution)/shard_map/while
  84.3 7.5 %copy-start.2 = (bf16[256,256]{1,0:T(8,128)(2,1)S(1)}, bf16[256,256]{1,0:T(8,128)(2,1)}, u32[]{:S(2)}) copy-start(bf16[256,256]{1,0:T(8,128)(2,1)} %get-tuple-element.447) | copy-start | bytes 393220 | tf_op jit(solution)/shard_map/while
  84.3 7.5 %copy-start.8 = (f32[256]{0:T(256)S(1)}, f32[256]{0:T(256)}, u32[]{:S(2)}) copy-start(f32[256]{0:T(256)} %get-tuple-element.457) | copy-start | bytes 3076 | tf_op jit(solution)/shard_map/while
  104.4 7.3 %copy-start.4 = (bf16[32,256]{1,0:T(8,128)(2,1)S(1)}, bf16[32,256]{1,0:T(8,128)(2,1)}, u32[]{:S(2)}) copy-start(bf16[32,256]{1,0:T(8,128)(2,1)} %get-tuple-element.454) | copy-start | bytes 49156 | tf_op jit(solution)/shard_map/while
  104.4 7.5 %copy-start.2 = (bf16[256,256]{1,0:T(8,128)(2,1)S(1)}, bf16[256,256]{1,0:T(8,128)(2,1)}, u32[]{:S(2)}) copy-start(bf16[256,256]{1,0:T(8,128)(2,1)} %get-tuple-element.447) | copy-start | bytes 393220 | tf_op jit(solution)/shard_map/while
  104.4 7.5 %copy-start.8 = (f32[256]{0:T(256)S(1)}, f32[256]{0:T(256)}, u32[]{:S(2)}) copy-start(f32[256]{0:T(256)} %get-tuple-element.457) | copy-start | bytes 3076 | tf_op jit(solution)/shard_map/while
  124.4 7.5 %copy-start.2 = (bf16[256,256]{1,0:T(8,128)(2,1)S(1)}, bf16[256,256]{1,0:T(8,128)(2,1)}, u32[]{:S(2)}) copy-start(bf16[256,256]{1,0:T(8,128)(2,1)} %get-tuple-element.447) | copy-start | bytes 393220 | tf_op jit(solution)/shard_map/while
  124.4 7.5 %copy-start.8 = (f32[256]{0:T(256)S(1)}, f32[256]{0:T(256)}, u32[]{:S(2)}) copy-start(f32[256]{0:T(256)} %get-tuple-element.457) | copy-start | bytes 3076 | tf_op jit(solution)/shard_map/while
  144.5 7.5 %copy-start.2 = (bf16[256,256]{1,0:T(8,128)(2,1)S(1)}, bf16[256,256]{1,0:T(8,128)(2,1)}, u32[]{:S(2)}) copy-start(bf16[256,256]{1,0:T(8,128)(2,1)} %get-tuple-element.447) | copy-start | bytes 393220 | tf_op jit(solution)/shard_map/while
  144.5 7.5 %copy-start.8 = (f32[256]{0:T(256)S(1)}, f32[256]{0:T(256)}, u32[]{:S(2)}) copy-start(f32[256]{0:T(256)} %get-tuple-element.457) | copy-start | bytes 3076 | tf_op jit(solution)/shard_map/while
  164.5 7.5 %copy-start.2 = (bf16[256,256]{1,0:T(8,128)(2,1)S(1)}, bf16[256,256]{1,0:T(8,128)(2,1)}, u32[]{:S(2)}) copy-start(bf16[256,256]{1,0:T(8,128)(2,1)} %get-tuple-element.447) | copy-start | bytes 393220 | tf_op jit(solution)/shard_map/while
  164.5 7.5 %copy-start.8 = (f32[256]{0:T(256)S(1)}, f32[256]{0:T(256)}, u32[]{:S(2)}) copy-start(f32[256]{0:T(256)} %get-tuple-element.457) | copy-start | bytes 3076 | tf_op jit(solution)/shard_map/while
  182.8 65.7 %copy-start.3 = (f32[256,256]{1,0:T(8,128)}, f32[256,256]{1,0:T(8,128)S(1)}, u32[]{:S(2)}) copy-start(f32[256,256]{1,0:T(8,128)S(1)} %get-tuple-element.126) | copy-start | bytes 786436
  (30 other events, 172.8 us)
Sparse Core Ops, SparseCore 0:
  9.6 11.4 all-gather.1
  248.6 92.3 all-reduce.3
where the time goes:
time: 352 us; the launch traced here: 350 us
  matrix products  132 us (38%)
  waiting for transfers between devices  99.3 us (28%)
  blocking collectives  61.6 us (18%)
  other arithmetic  35.4 us (10%)
  between operations  14.2 us (4%)
  local copies, waits for them, and re-layouts  4.24 us (1%)
    psum x1, waiting for transfers between devices, local(): lax.psum((grads[0], grads[1], grads[2], grads[3], grads[4]), ('slices', '...  90.4 us
    psum x1, blocking collectives, local(): lax.psum((grads[0], grads[1], grads[2], grads[3], grads[4]), ('slices', '...  57.3 us
    dot_general x8, matrix products, one_slice(): jnp.einsum('ck,kij->cij', embed_weight, features, precision=HIGH)  36.2 us
    dot_general x8, matrix products, one_slice(): jnp.einsum('cij,kij->ck', act_low, pair_in, preferred_element_type=jnp.fl...  27.9 us
    dot_general x8, matrix products, one_slice(): jnp.einsum('ck,kij->cij', pair_weight, pair_in, preferred_element_type=jn...  21.9 us
    dot_general x8, matrix products, one_slice(): jnp.dot(pre_grad, one_weight.T, preferred_element_type=jnp.float32)  13.5 us
    dynamic_update_slice x8, other arithmetic, local(): lax.scan(one_slice, start, inputs)  11.9 us
    reduce_sum x8, other arithmetic, one_slice(): bias_term = jnp.sum(act_grad, axis=(1, 2))  11.8 us
  transfers between devices with their start and end apart: 3, of which 2 were waited for; matrix products, arithmetic and copies ran while one was open for 48% of the time, Pallas kernels for 0%

commit v1 on v0

--- a/solution.py
+++ b/solution.py
@@ -102,7 +102,9 @@
     hidden_grad = (partial_grad + mean_back[:, None, :] / total_count).astype(jnp.bfloat16)
     mean_term = jnp.dot(mean_rows.astype(jnp.float32).T, column_parts, precision=HIGH)
     grads = (totals[0], totals[1], totals[2], totals[3], mean_term)
-    grads = lax.psum((grads[0], grads[1], grads[2], grads[3], grads[4]), ("slices", "ering"))
+    grads = jax.lax.psum(
+        jax.lax.psum((grads[0], grads[1], grads[2], grads[3], grads[4]), "ering"), "slices"
+    )
     drift = jnp.einsum(
         "cd,sid->csi", drift_weight.astype(jnp.float32), updated.astype(jnp.float32), precision=HIGH
     )

time: 352 us -> 310 us (0.88)
  blocking collectives: 61.6 us -> 36.1 us
  waiting for transfers between devices: 99.3 us -> 80.5 us
    psum x1, blocking collectives: 57.3 us -> 30.6 us  [local(): jax.lax.psum(jax.lax.psum((grads[0], grads[1], grads[2], grads[3], grads[...]
    psum x1 -> x2, waiting for transfers between devices: 90.4 us -> 71.5 us  [the longest x1 71.5 us: local(): jax.lax.psum(jax.lax.psum((grads[0], grads[1], grads[2], grads[3], grads[...]
  transfers between devices with their start and end apart: 3 -> 4, of which waited for: 2 -> 2; matrix products, arithmetic and copies ran while one was open for 48% -> 56% of each run, Pallas kernels for 0% -> 0%
where the time goes in v1:
time: 310 us; the launch traced here: 305 us
  matrix products  132 us (43%)
  waiting for transfers between devices  80.5 us (26%)
  blocking collectives  36.1 us (12%)
  other arithmetic  35.4 us (11%)
  between operations  13.9 us (4%)
  local copies, waits for them, and re-layouts  4.24 us (1%)
    psum x1, waiting for transfers between devices, local(): jax.lax.psum(jax.lax.psum((grads[0], grads[1], grads[2], grads[3], grads[...  71.5 us
    dot_general x8, matrix products, one_slice(): jnp.einsum('ck,kij->cij', embed_weight, features, precision=HIGH)  36.2 us
    psum x1, blocking collectives, local(): jax.lax.psum(jax.lax.psum((grads[0], grads[1], grads[2], grads[3], grads[...  30.6 us
    dot_general x8, matrix products, one_slice(): jnp.einsum('cij,kij->ck', act_low, pair_in, preferred_element_type=jnp.fl...  28 us
    dot_general x8, matrix products, one_slice(): jnp.einsum('ck,kij->cij', pair_weight, pair_in, preferred_element_type=jn...  22 us
    dot_general x8, matrix products, one_slice(): jnp.dot(pre_grad, one_weight.T, preferred_element_type=jnp.float32)  13.6 us
    dynamic_update_slice x8, other arithmetic, local(): lax.scan(one_slice, start, inputs)  11.9 us
    reduce_sum x8, other arithmetic, one_slice(): bias_term = jnp.sum(act_grad, axis=(1, 2))  11.8 us
  transfers between devices with their start and end apart: 4, of which 2 were waited for; matrix products, arithmetic and copies ran while one was open for 56% of the time, Pallas kernels for 0%

profile of v1, /device:TPU:1, one launch (start us, length us, event | category | flops | bytes accessed | tf_op | source)
XLA Modules:
  0.0 305.2 jit_solution(2375710485199730243)
XLA Ops:
  12.8 8.3 %all-gather.2.cloned.1.call-done = bf16[8,256,256]{2,1,0:T(8,128)(2,1)} async-done(((bf16[8,128,256]{2,1,0:T(8,128)(2,1)}), bf16[8,256,256]{2,1,0:T(8,128)(2,1)}) %all-gather.2.cloned.1.call-update) | async-done | bytes 1048592 | tf_op jit(solution)/shard_map/all_gather | solution.py:36
  22.5 160.5 %while.23 = (s32[]{:T(128)}, f32[32,32]{1,0:T(8,128)S(1)}, f32[32]{0:T(128)S(1)}, f32[256,256]{1,0:T(8,128)S(1)}, f32[32,256]{1,0:T(8,128)S(1)}, /*index=5*/bf16...) while((s32[]{:T(128)}, f32[32,32]{1,0:T(8,128)S(1)}, ...), condition=%wide.region_6.7_spmd.clone, body=%wide.region_1.6_spmd.clone.sunk | while | flops 259163936 | bytes 40384416 | solution.py:99
  24.3 4.5 %tanh_convert_fusion.2 = bf16[128,256,32]{1,2,0:T(8,128)(2,1)S(1)} fusion(f32[32]{0:T(128)} %get-tuple-element.457, f32[1,128,256]{2,0,1:T(1,128)S(1)} %copy.37, f32[3,128,256]{2,0,1:T(4,128)S(1)} %get-tuple-element.391, f32[32,4]{0,1:T(4,128)} %get-tuple-element.456), kind=kOutput, calls=%fused_computation.6.clone.1 | convolution fusion | flops 52559872 | bytes 2622080 | tf_op jit(solution)/shard_map/while/body/eval_jaxpr/ck,kij->cij/dot_general | solution.py:45
  33.3 3.5 %fusion.115 = f32[32,32]{1,0:T(8,128)S(1)} fusion(bf16[128,256,32]{1,2,0:T(8,128)(2,1)S(1)} %tanh_convert_fusion.2, f32[128,256,32]{1,2,0:T(8,128)} %get-tuple-element.392, f32[32,128]{0,1:T(8,128)S(1)} %copy.38, f32[32]{0:T(128)S(1)} %copy-done.7, f32[32,32]{1,0:T(8,128)S(1)} %get-tuple-element.421, pred[]{:T(512)S(6)} %compare.3), kind=kOutput, calls=%fused_computation.27.clone.1 | convolution fusion | flops 72353792 | bytes 6316161 | tf_op jit(solution)/shard_map/while/body/eval_jaxpr/cij,kij->ck/dot_general | solution.py:71
  44.3 4.5 %tanh_convert_fusion.2 = bf16[128,256,32]{1,2,0:T(8,128)(2,1)S(1)} fusion(f32[32]{0:T(128)} %get-tuple-element.457, f32[1,128,256]{2,0,1:T(1,128)S(1)} %copy.37, f32[3,128,256]{2,0,1:T(4,128)S(1)} %get-tuple-element.391, f32[32,4]{0,1:T(4,128)} %get-tuple-element.456), kind=kOutput, calls=%fused_computation.6.clone.1 | convolution fusion | flops 52559872 | bytes 2622080 | tf_op jit(solution)/shard_map/while/body/eval_jaxpr/ck,kij->cij/dot_general | solution.py:45
  48.9 2.8 fusion.111
  53.3 3.5 %fusion.115 = f32[32,32]{1,0:T(8,128)S(1)} fusion(bf16[128,256,32]{1,2,0:T(8,128)(2,1)S(1)} %tanh_convert_fusion.2, f32[128,256,32]{1,2,0:T(8,128)} %get-tuple-element.392, f32[32,128]{0,1:T(8,128)S(1)} %copy.38, f32[32]{0:T(128)S(1)} %copy-done.7, f32[32,32]{1,0:T(8,128)S(1)} %get-tuple-element.421, pred[]{:T(512)S(6)} %compare.3), kind=kOutput, calls=%fused_computation.27.clone.1 | convolution fusion | flops 72353792 | bytes 6316161 | tf_op jit(solution)/shard_map/while/body/eval_jaxpr/cij,kij->ck/dot_general | solution.py:71
  64.4 4.5 %tanh_convert_fusion.2 = bf16[128,256,32]{1,2,0:T(8,128)(2,1)S(1)} fusion(f32[32]{0:T(128)} %get-tuple-element.457, f32[1,128,256]{2,0,1:T(1,128)S(1)} %copy.37, f32[3,128,256]{2,0,1:T(4,128)S(1)} %get-tuple-element.391, f32[32,4]{0,1:T(4,128)} %get-tuple-element.456), kind=kOutput, calls=%fused_computation.6.clone.1 | convolution fusion | flops 52559872 | bytes 2622080 | tf_op jit(solution)/shard_map/while/body/eval_jaxpr/ck,kij->cij/dot_general | solution.py:45
  68.9 2.8 fusion.111
  73.4 3.5 %fusion.115 = f32[32,32]{1,0:T(8,128)S(1)} fusion(bf16[128,256,32]{1,2,0:T(8,128)(2,1)S(1)} %tanh_convert_fusion.2, f32[128,256,32]{1,2,0:T(8,128)} %get-tuple-element.392, f32[32,128]{0,1:T(8,128)S(1)} %copy.38, f32[32]{0:T(128)S(1)} %copy-done.7, f32[32,32]{1,0:T(8,128)S(1)} %get-tuple-element.421, pred[]{:T(512)S(6)} %compare.3), kind=kOutput, calls=%fused_computation.27.clone.1 | convolution fusion | flops 72353792 | bytes 6316161 | tf_op jit(solution)/shard_map/while/body/eval_jaxpr/cij,kij->ck/dot_general | solution.py:71
  84.4 4.5 %tanh_convert_fusion.2 = bf16[128,256,32]{1,2,0:T(8,128)(2,1)S(1)} fusion(f32[32]{0:T(128)} %get-tuple-element.457, f32[1,128,256]{2,0,1:T(1,128)S(1)} %copy.37, f32[3,128,256]{2,0,1:T(4,128)S(1)} %get-tuple-element.391, f32[32,4]{0,1:T(4,128)} %get-tuple-element.456), kind=kOutput, calls=%fused_computation.6.clone.1 | convolution fusion | flops 52559872 | bytes 2622080 | tf_op jit(solution)/shard_map/while/body/eval_jaxpr/ck,kij->cij/dot_general | solution.py:45
  89.0 2.8 fusion.111
  93.4 3.5 %fusion.115 = f32[32,32]{1,0:T(8,128)S(1)} fusion(bf16[128,256,32]{1,2,0:T(8,128)(2,1)S(1)} %tanh_convert_fusion.2, f32[128,256,32]{1,2,0:T(8,128)} %get-tuple-element.392, f32[32,128]{0,1:T(8,128)S(1)} %copy.38, f32[32]{0:T(128)S(1)} %copy-done.7, f32[32,32]{1,0:T(8,128)S(1)} %get-tuple-element.421, pred[]{:T(512)S(6)} %compare.3), kind=kOutput, calls=%fused_computation.27.clone.1 | convolution fusion | flops 72353792 | bytes 6316161 | tf_op jit(solution)/shard_map/while/body/eval_jaxpr/cij,kij->ck/dot_general | solution.py:71
  104.5 4.5 %tanh_convert_fusion.2 = bf16[128,256,32]{1,2,0:T(8,128)(2,1)S(1)} fusion(f32[32]{0:T(128)} %get-tuple-element.457, f32[1,128,256]{2,0,1:T(1,128)S(1)} %copy.37, f32[3,128,256]{2,0,1:T(4,128)S(1)} %get-tuple-element.391, f32[32,4]{0,1:T(4,128)} %get-tuple-element.456), kind=kOutput, calls=%fused_computation.6.clone.1 | convolution fusion | flops 52559872 | bytes 2622080 | tf_op jit(solution)/shard_map/while/body/eval_jaxpr/ck,kij->cij/dot_general | solution.py:45
  113.5 3.5 %fusion.115 = f32[32,32]{1,0:T(8,128)S(1)} fusion(bf16[128,256,32]{1,2,0:T(8,128)(2,1)S(1)} %tanh_convert_fusion.2, f32[128,256,32]{1,2,0:T(8,128)} %get-tuple-element.392, f32[32,128]{0,1:T(8,128)S(1)} %copy.38, f32[32]{0:T(128)S(1)} %copy-done.7, f32[32,32]{1,0:T(8,128)S(1)} %get-tuple-element.421, pred[]{:T(512)S(6)} %compare.3), kind=kOutput, calls=%fused_computation.27.clone.1 | convolution fusion | flops 72353792 | bytes 6316161 | tf_op jit(solution)/shard_map/while/body/eval_jaxpr/cij,kij->ck/dot_general | solution.py:71
  124.5 4.5 %tanh_convert_fusion.2 = bf16[128,256,32]{1,2,0:T(8,128)(2,1)S(1)} fusion(f32[32]{0:T(128)} %get-tuple-element.457, f32[1,128,256]{2,0,1:T(1,128)S(1)} %copy.37, f32[3,128,256]{2,0,1:T(4,128)S(1)} %get-tuple-element.391, f32[32,4]{0,1:T(4,128)} %get-tuple-element.456), kind=kOutput, calls=%fused_computation.6.clone.1 | convolution fusion | flops 52559872 | bytes 2622080 | tf_op jit(solution)/shard_map/while/body/eval_jaxpr/ck,kij->cij/dot_general | solution.py:45
  133.5 3.5 %fusion.115 = f32[32,32]{1,0:T(8,128)S(1)} fusion(bf16[128,256,32]{1,2,0:T(8,128)(2,1)S(1)} %tanh_convert_fusion.2, f32[128,256,32]{1,2,0:T(8,128)} %get-tuple-element.392, f32[32,128]{0,1:T(8,128)S(1)} %copy.38, f32[32]{0:T(128)S(1)} %copy-done.7, f32[32,32]{1,0:T(8,128)S(1)} %get-tuple-element.421, pred[]{:T(512)S(6)} %compare.3), kind=kOutput, calls=%fused_computation.27.clone.1 | convolution fusion | flops 72353792 | bytes 6316161 | tf_op jit(solution)/shard_map/while/body/eval_jaxpr/cij,kij->ck/dot_general | solution.py:71
  144.6 4.5 %tanh_convert_fusion.2 = bf16[128,256,32]{1,2,0:T(8,128)(2,1)S(1)} fusion(f32[32]{0:T(128)} %get-tuple-element.457, f32[1,128,256]{2,0,1:T(1,128)S(1)} %copy.37, f32[3,128,256]{2,0,1:T(4,128)S(1)} %get-tuple-element.391, f32[32,4]{0,1:T(4,128)} %get-tuple-element.456), kind=kOutput, calls=%fused_computation.6.clone.1 | convolution fusion | flops 52559872 | bytes 2622080 | tf_op jit(solution)/shard_map/while/body/eval_jaxpr/ck,kij->cij/dot_general | solution.py:45
  153.6 3.5 %fusion.115 = f32[32,32]{1,0:T(8,128)S(1)} fusion(bf16[128,256,32]{1,2,0:T(8,128)(2,1)S(1)} %tanh_convert_fusion.2, f32[128,256,32]{1,2,0:T(8,128)} %get-tuple-element.392, f32[32,128]{0,1:T(8,128)S(1)} %copy.38, f32[32]{0:T(128)S(1)} %copy-done.7, f32[32,32]{1,0:T(8,128)S(1)} %get-tuple-element.421, pred[]{:T(512)S(6)} %compare.3), kind=kOutput, calls=%fused_computation.27.clone.1 | convolution fusion | flops 72353792 | bytes 6316161 | tf_op jit(solution)/shard_map/while/body/eval_jaxpr/cij,kij->ck/dot_general | solution.py:71
  164.6 4.5 %tanh_convert_fusion.2 = bf16[128,256,32]{1,2,0:T(8,128)(2,1)S(1)} fusion(f32[32]{0:T(128)} %get-tuple-element.457, f32[1,128,256]{2,0,1:T(1,128)S(1)} %copy.37, f32[3,128,256]{2,0,1:T(4,128)S(1)} %get-tuple-element.391, f32[32,4]{0,1:T(4,128)} %get-tuple-element.456), kind=kOutput, calls=%fused_computation.6.clone.1 | convolution fusion | flops 52559872 | bytes 2622080 | tf_op jit(solution)/shard_map/while/body/eval_jaxpr/ck,kij->cij/dot_general | solution.py:45
  173.7 3.5 %fusion.115 = f32[32,32]{1,0:T(8,128)S(1)} fusion(bf16[128,256,32]{1,2,0:T(8,128)(2,1)S(1)} %tanh_convert_fusion.2, f32[128,256,32]{1,2,0:T(8,128)} %get-tuple-element.392, f32[32,128]{0,1:T(8,128)S(1)} %copy.38, f32[32]{0:T(128)S(1)} %copy-done.7, f32[32,32]{1,0:T(8,128)S(1)} %get-tuple-element.421, pred[]{:T(512)S(6)} %compare.3), kind=kOutput, calls=%fused_computation.27.clone.1 | convolution fusion | flops 72353792 | bytes 6316161 | tf_op jit(solution)/shard_map/while/body/eval_jaxpr/cij,kij->ck/dot_general | solution.py:71
  186.0 3.7 %all-reduce.2 = (f32[8,256]{1,0:T(8,128)S(1)}, f32[32,32]{1,0:T(8,128)S(1)}, f32[32]{0:T(128)S(1)}, f32[32,256]{1,0:T(8,128)S(1)}) all-reduce(f32[8,256]{1,0:T(8,128)S(1)} %get-tuple-element.123, f32[32,32]{1,0:T(8,128)S(1)} %get-tuple-element.124, ...), channel_id=1, replica_groups=mesh['groups'=2,'slices'=8,'ering'=2] {'ering'}, use_global_device_ids=true, to_apply=%region_7.8 | all-reduce | flops 11296 | bytes 90368 | tf_op jit(solution)/shard_map/psum | solution.py:100
  189.8 30.6 %all-reduce = (f32[32,32]{1,0:T(8,128)S(1)}, f32[32]{0:T(128)S(1)}, f32[32,256]{1,0:T(8,128)S(1)}) all-reduce(f32[32,32]{1,0:T(8,128)S(1)} %get-tuple-element.242, f32[32]{0:T(128)S(1)} %get-tuple-element.243, f32[32,256]{1,0:T(8,128)S(1)} %get-tuple-element.244), channel_id=1, replica_groups=mesh['groups'=2,'slices'=8,'ering'=2] {'slices'}, use_global_device_ids=true, to_apply=%region_10.11 | all-reduce | flops 9248 | bytes 73984 | tf_op jit(solution)/shard_map/psum | solution.py:105
  225.4 71.5 %all-reduce.7.cloned.1.call-done = (f32[256,256]{1,0:T(8,128)}, f32[256,256]{1,0:T(8,128)}) async-done(((f32[256,256]{1,0:T(8,128)}, f32[256,256]{1,0:T(8,128)}), (f32[256,256]{1,0:T(8,128)}, f32[256,256]{1,0:T(8,128)})) %all-reduce.7.cloned.1.call-update) | async-done | bytes 524304 | tf_op jit(solution)/shard_map/psum | solution.py:105
  (276 shorter events, 103.6 us)
Async XLA Ops:
  7.2 176.9 %copy-start = (bf16[3,256]{1,0:T(4,128)(2,1)S(1)}, bf16[3,256]{1,0:T(4,128)(2,1)}, u32[]{:S(2)}) copy-start(bf16[3,256]{1,0:T(4,128)(2,1)} %param.25) | copy-start | bytes 4612
  7.2 13.9 %all-gather.2.cloned.1.call-start = ((), (), s32[]{:S(2)}) async-start(), calls=%async_computation | async-start | bytes 1572864 | tf_op jit(solution)/shard_map/all_gather | solution.py:36
  7.9 213.6 %all-reduce.9.cloned.1.call-start = ((), (), s32[]{:S(2)}) async-start(), calls=%async_computation.2 | async-start | bytes 1048576 | tf_op jit(solution)/shard_map/psum | solution.py:106
  8.7 175.4 %collective-permute-start = (f32[3,1,128]{2,0,1:T(4,128)S(1)}, f32[3,1,128]{2,0,1:T(4,128)S(1)}, u32[]{:S(2)}, u32[]{:S(2)}) collective-permute-start(f32[3,1,128]{2,0,1:T(4,128)S(1)} %slice.9), channel_id=1, source_target_pairs={{2,0},{4,2},{6,4},{8,6},{10,8},{12,10},{14,12},{3,1},{5,3},{7,5},{... | collective-permute-start | bytes 4616 | tf_op jit(solution)/shard_map/ppermute | solution.py:14
  22.5 161.6 %copy-start.6 = (f32[3,8,128]{2,1,0:T(8,128)S(1)}, f32[3,8,128]{2,1,0:T(8,128)}, u32[]{:S(2)}) copy-start(f32[3,8,128]{2,1,0:T(8,128)} %param.14) | copy-start | bytes 36868
  24.2 7.5 %copy-start.2 = (bf16[256,256]{1,0:T(8,128)(2,1)S(1)}, bf16[256,256]{1,0:T(8,128)(2,1)}, u32[]{:S(2)}) copy-start(bf16[256,256]{1,0:T(8,128)(2,1)} %get-tuple-element.453) | copy-start | bytes 393220 | tf_op jit(solution)/shard_map/while
  24.2 7.5 %copy-start.8 = (f32[256]{0:T(256)S(1)}, f32[256]{0:T(256)}, u32[]{:S(2)}) copy-start(f32[256]{0:T(256)} %get-tuple-element.463) | copy-start | bytes 3076 | tf_op jit(solution)/shard_map/while
  44.3 7.5 %copy-start.2 = (bf16[256,256]{1,0:T(8,128)(2,1)S(1)}, bf16[256,256]{1,0:T(8,128)(2,1)}, u32[]{:S(2)}) copy-start(bf16[256,256]{1,0:T(8,128)(2,1)} %get-tuple-element.453) | copy-start | bytes 393220 | tf_op jit(solution)/shard_map/while
  44.3 7.5 %copy-start.8 = (f32[256]{0:T(256)S(1)}, f32[256]{0:T(256)}, u32[]{:S(2)}) copy-start(f32[256]{0:T(256)} %get-tuple-element.463) | copy-start | bytes 3076 | tf_op jit(solution)/shard_map/while
  64.3 7.5 %copy-start.2 = (bf16[256,256]{1,0:T(8,128)(2,1)S(1)}, bf16[256,256]{1,0:T(8,128)(2,1)}, u32[]{:S(2)}) copy-start(bf16[256,256]{1,0:T(8,128)(2,1)} %get-tuple-element.453) | copy-start | bytes 393220 | tf_op jit(solution)/shard_map/while
  64.3 7.5 %copy-start.8 = (f32[256]{0:T(256)S(1)}, f32[256]{0:T(256)}, u32[]{:S(2)}) copy-start(f32[256]{0:T(256)} %get-tuple-element.463) | copy-start | bytes 3076 | tf_op jit(solution)/shard_map/while
  84.4 7.5 %copy-start.2 = (bf16[256,256]{1,0:T(8,128)(2,1)S(1)}, bf16[256,256]{1,0:T(8,128)(2,1)}, u32[]{:S(2)}) copy-start(bf16[256,256]{1,0:T(8,128)(2,1)} %get-tuple-element.453) | copy-start | bytes 393220 | tf_op jit(solution)/shard_map/while
  84.4 7.5 %copy-start.8 = (f32[256]{0:T(256)S(1)}, f32[256]{0:T(256)}, u32[]{:S(2)}) copy-start(f32[256]{0:T(256)} %get-tuple-element.463) | copy-start | bytes 3076 | tf_op jit(solution)/shard_map/while
  104.4 7.5 %copy-start.2 = (bf16[256,256]{1,0:T(8,128)(2,1)S(1)}, bf16[256,256]{1,0:T(8,128)(2,1)}, u32[]{:S(2)}) copy-start(bf16[256,256]{1,0:T(8,128)(2,1)} %get-tuple-element.453) | copy-start | bytes 393220 | tf_op jit(solution)/shard_map/while
  104.5 7.5 %copy-start.8 = (f32[256]{0:T(256)S(1)}, f32[256]{0:T(256)}, u32[]{:S(2)}) copy-start(f32[256]{0:T(256)} %get-tuple-element.463) | copy-start | bytes 3076 | tf_op jit(solution)/shard_map/while
  124.5 7.5 %copy-start.2 = (bf16[256,256]{1,0:T(8,128)(2,1)S(1)}, bf16[256,256]{1,0:T(8,128)(2,1)}, u32[]{:S(2)}) copy-start(bf16[256,256]{1,0:T(8,128)(2,1)} %get-tuple-element.453) | copy-start | bytes 393220 | tf_op jit(solution)/shard_map/while
  124.5 7.5 %copy-start.8 = (f32[256]{0:T(256)S(1)}, f32[256]{0:T(256)}, u32[]{:S(2)}) copy-start(f32[256]{0:T(256)} %get-tuple-element.463) | copy-start | bytes 3076 | tf_op jit(solution)/shard_map/while
  144.6 7.3 %copy-start.4 = (bf16[32,256]{1,0:T(8,128)(2,1)S(1)}, bf16[32,256]{1,0:T(8,128)(2,1)}, u32[]{:S(2)}) copy-start(bf16[32,256]{1,0:T(8,128)(2,1)} %get-tuple-element.460) | copy-start | bytes 49156 | tf_op jit(solution)/shard_map/while
  144.6 7.5 %copy-start.2 = (bf16[256,256]{1,0:T(8,128)(2,1)S(1)}, bf16[256,256]{1,0:T(8,128)(2,1)}, u32[]{:S(2)}) copy-start(bf16[256,256]{1,0:T(8,128)(2,1)} %get-tuple-element.453) | copy-start | bytes 393220 | tf_op jit(solution)/shard_map/while
  144.6 7.5 %copy-start.8 = (f32[256]{0:T(256)S(1)}, f32[256]{0:T(256)}, u32[]{:S(2)}) copy-start(f32[256]{0:T(256)} %get-tuple-element.463) | copy-start | bytes 3076 | tf_op jit(solution)/shard_map/while
  164.6 7.3 %copy-start.4 = (bf16[32,256]{1,0:T(8,128)(2,1)S(1)}, bf16[32,256]{1,0:T(8,128)(2,1)}, u32[]{:S(2)}) copy-start(bf16[32,256]{1,0:T(8,128)(2,1)} %get-tuple-element.460) | copy-start | bytes 49156 | tf_op jit(solution)/shard_map/while
  164.6 7.5 %copy-start.2 = (bf16[256,256]{1,0:T(8,128)(2,1)S(1)}, bf16[256,256]{1,0:T(8,128)(2,1)}, u32[]{:S(2)}) copy-start(bf16[256,256]{1,0:T(8,128)(2,1)} %get-tuple-element.453) | copy-start | bytes 393220 | tf_op jit(solution)/shard_map/while
  164.6 7.5 %copy-start.8 = (f32[256]{0:T(256)S(1)}, f32[256]{0:T(256)}, u32[]{:S(2)}) copy-start(f32[256]{0:T(256)} %get-tuple-element.463) | copy-start | bytes 3076 | tf_op jit(solution)/shard_map/while
  184.0 112.8 %all-reduce.7.cloned.1.call-start = ((), (), s32[]{:S(2)}) async-start(), calls=%async_computation.1 | async-start | bytes 1048576 | tf_op jit(solution)/shard_map/psum | solution.py:105
  (31 other events, 173.9 us)
Sparse Core Ops, SparseCore 0:
  9.6 11.4 all-gather.1
  184.1 19.9 all-reduce.8
  221.7 75.0 all-reduce.6
